TPU v7x, 32 devices: a whole 2x2x4 slice. The times are simulated.
32 devices in a mesh: rows: 16 (over z, y, core), cent: 2 (over x).
Axes of the slice: x: 2, y: 2, z: 4, core: 2. Of those that a mesh axis runs over, the one named last changes fastest.
Arguments:
- vectors: bfloat16 [32768, 1024], P('rows'), may hold values from -40 to 40
- centroids: bfloat16 [1024, 4096], P('rows', 'cent'), may hold values from -8 to 8
Outputs:
- centroid_sums: float32 [1024, 4096], P('rows', 'cent')
All inputs are finite; a program needn't handle non-finite values.
Results may differ from a plain program's by a relative error of at most 0.0017.
Values may be sent and summed in bfloat16 or wider, within the bound.
A program may use at most 64 MiB of HBM per device.

v0:
```python
import math
import jax
import jax.numpy as jnp
from jax import lax
from jax.sharding import PartitionSpec as P

K = 4096
ITERS = 3
sharpness = 3.0


def on_device(vectors, centroids):
    row_count = vectors.shape[0]
    width = vectors.shape[1]
    window = vectors
    scores = jnp.dot(
        window,
        lax.all_gather(centroids, "rows", axis=0, tiled=True),
        preferred_element_type=jnp.float32,
    )
    scores = scores * (sharpness / math.sqrt(width))
    row_top = lax.pmax(jnp.max(scores, axis=1), "cent")
    numerator = jnp.exp(scores - row_top[:, None])
    row_total = lax.psum(jnp.sum(numerator, axis=1), "cent")
    balanced = numerator / row_total[:, None]
    target = row_count * lax.axis_size("rows") / K
    for iteration in range(ITERS):
        column_sum = jnp.sum(balanced, axis=0)
        column_mass = lax.psum(column_sum, "rows")
        column_scale = target / column_mass
        balanced = balanced * column_scale[None, :]
        row_mass = lax.psum(jnp.sum(balanced, axis=1), "cent")
        balanced = balanced / row_mass[:, None]
    weights = balanced.astype(jnp.bfloat16)
    factor = K / (row_count * lax.axis_size("rows"))
    window = vectors
    mine = lax.psum_scatter(
        lax.dot_general(
            window, weights, (((0,), (0,)), ((), ())), preferred_element_type=jnp.float32
        ),
        "rows",
        scatter_dimension=0,
        tiled=True,
    )
    return mine * factor


def solution(mesh):
    return jax.shard_map(
        on_device,
        mesh=mesh,
        in_specs=(P("rows", None), P("rows", "cent")),
        out_specs=P("rows", "cent"),
        check_vma=False,
    )
```

profile of v0, /device:TPU:0, one launch (start us, length us, event | category | flops | bytes accessed | tf_op | source)
XLA Modules:
  0.0 386.2 jit_solution(11446826470317669100)
XLA Ops:
  6.5 0.0 all-gather.2.cloned.1.call-start
  6.5 0.7 all-gather.2.cloned.1.call-update
  7.3 0.0 reduce-scatter.4.cloned.1.call-start
  7.3 55.3 %all-gather.2.cloned.1.call-done = bf16[1024,2048]{1,0:T(8,128)(2,1)} async-done(((bf16[64,2048]{1,0:T(8,128)(2,1)}), bf16[1024,2048]{1,0:T(8,128)(2,1)}) %all-gather.2.cloned.1.call-update) | async-done | bytes 4194320 | tf_op jit(solution)/shard_map/all_gather | solution.py:18
  62.6 15.2 %multiply_reduce_fusion.3 = (f32[2048]{0:T(1024)S(1)}, f32[2048,2048]{0,1:T(8,128)}) fusion(bf16[2048,1024]{1,0:T(8,128)(2,1)} %param.2, bf16[1024,2048]{1,0:T(8,128)(2,1)} %all-gather.2.cloned.1.call-done), kind=kOutput, calls=%fused_computation.7 | convolution fusion | flops 8598321152 | bytes 25174016 | tf_op jit(solution)/shard_map/dot_general | solution.py:16
  77.9 5.0 %pmax.7 = f32[2048]{0:T(1024)S(1)} all-reduce(f32[2048]{0:T(1024)S(1)} %get-tuple-element.7), channel_id=1, replica_groups=mesh['rows'=16,'cent'=2] {'cent'}, use_global_device_ids=true, to_apply=%region_1.0 | all-reduce | flops 2048 | bytes 16384 | tf_op jit(solution)/shard_map/pmax | solution.py:22
  82.8 8.5 %fusion.1 = f32[2048]{0:T(1024)S(1)} fusion(f32[2048,2048]{0,1:T(8,128)} %get-tuple-element.8, f32[2048]{0:T(1024)S(1)} %pmax.7), kind=kLoop, calls=%fused_computation.9 | loop fusion | flops 12580864 | bytes 16793600 | tf_op jit(solution)/shard_map/reduce_sum | solution.py:24
  91.4 5.0 %psum.49 = f32[2048]{0:T(1024)S(1)} all-reduce(f32[2048]{0:T(1024)S(1)} %fusion.1), channel_id=1, replica_groups=mesh['rows'=16,'cent'=2] {'cent'}, use_global_device_ids=true, to_apply=%region_3.0 | all-reduce | flops 2048 | bytes 16384 | tf_op jit(solution)/shard_map/psum | solution.py:24
  96.4 7.7 %fusion.4 = f32[2048]{0:T(1024)S(1)} fusion(f32[2048]{0:T(1024)S(1)} %psum.49, f32[2048]{0:T(1024)S(1)} %pmax.7, f32[2048,2048]{0,1:T(8,128)} %get-tuple-element.8), kind=kLoop, calls=%fused_computation.16 | loop fusion | flops 16775168 | bytes 16801792 | tf_op jit(solution)/shard_map/reduce_sum | solution.py:28
  104.1 30.0 %psum.50 = f32[2048]{0:T(1024)S(1)} all-reduce(f32[2048]{0:T(1024)S(1)} %fusion.4), channel_id=1, replica_groups=mesh['rows'=16,'cent'=2] {'rows'}, use_global_device_ids=true, to_apply=%region_5.0 | all-reduce | flops 2048 | bytes 16384 | tf_op jit(solution)/shard_map/psum | solution.py:29
  134.1 8.1 %multiply_reduce_fusion.2 = f32[2048]{0:T(1024)S(1)} fusion(f32[2048]{0:T(1024)S(1)} %broadcast_divide_fusion.2, f32[2048]{0:T(1024)S(1)} %psum.49, f32[2048]{0:T(1024)S(1)} %pmax.7, f32[2048,2048]{0,1:T(8,128)} %get-tuple-element.8), kind=kLoop, calls=%fused_computation.6 | loop fusion | flops 20969472 | bytes 16809984 | tf_op jit(solution)/shard_map/reduce_sum | solution.py:32
  142.2 5.0 %psum.51 = f32[2048]{0:T(1024)S(1)} all-reduce(f32[2048]{0:T(1024)S(1)} %multiply_reduce_fusion.2), channel_id=1, replica_groups=mesh['rows'=16,'cent'=2] {'cent'}, use_global_device_ids=true, to_apply=%region_7.0 | all-reduce | flops 2048 | bytes 16384 | tf_op jit(solution)/shard_map/psum | solution.py:32
  147.2 13.1 %fusion.6 = (f32[2048]{0:T(1024)S(1)}, f32[2048,2048]{0,1:T(8,128)}) fusion(f32[2048]{0:T(1024)S(1)} %psum.51, f32[2048]{0:T(1024)S(1)} %broadcast_divide_fusion.2, f32[2048]{0:T(1024)S(1)} %psum.49, f32[2048]{0:T(1024)S(1)} %pmax.7, f32[2048,2048]{0,1:T(8,128)} %get-tuple-element.8), kind=kLoop, calls=%fused_computation.18 | loop fusion | flops 25163776 | bytes 33595392 | tf_op jit(solution)/shard_map/reduce_sum | solution.py:28
  160.3 30.2 %psum.52 = f32[2048]{0:T(1024)S(1)} all-reduce(f32[2048]{0:T(1024)S(1)} %get-tuple-element.5), channel_id=1, replica_groups=mesh['rows'=16,'cent'=2] {'rows'}, use_global_device_ids=true, to_apply=%region_9.0 | all-reduce | flops 2048 | bytes 16384 | tf_op jit(solution)/shard_map/psum | solution.py:29
  190.5 6.9 %multiply_reduce_fusion.1 = f32[2048]{0:T(1024)S(1)} fusion(f32[2048,2048]{0,1:T(8,128)} %get-tuple-element.6, f32[2048]{0:T(1024)S(1)} %broadcast_divide_fusion.1), kind=kLoop, calls=%fused_computation.4 | loop fusion | flops 8386560 | bytes 16793600 | tf_op jit(solution)/shard_map/reduce_sum | solution.py:32
  197.4 5.0 %psum.53 = f32[2048]{0:T(1024)S(1)} all-reduce(f32[2048]{0:T(1024)S(1)} %multiply_reduce_fusion.1), channel_id=1, replica_groups=mesh['rows'=16,'cent'=2] {'cent'}, use_global_device_ids=true, to_apply=%region_11.0 | all-reduce | flops 2048 | bytes 16384 | tf_op jit(solution)/shard_map/psum | solution.py:32
  202.5 7.1 %fusion.5 = f32[2048]{0:T(1024)S(1)} fusion(f32[2048]{0:T(1024)S(1)} %psum.53, f32[2048,2048]{0,1:T(8,128)} %get-tuple-element.6, f32[2048]{0:T(1024)S(1)} %broadcast_divide_fusion.1), kind=kLoop, calls=%fused_computation.17 | loop fusion | flops 12580864 | bytes 16801792 | tf_op jit(solution)/shard_map/reduce_sum | solution.py:28
  209.6 30.0 %psum.54 = f32[2048]{0:T(1024)S(1)} all-reduce(f32[2048]{0:T(1024)S(1)} %fusion.5), channel_id=1, replica_groups=mesh['rows'=16,'cent'=2] {'rows'}, use_global_device_ids=true, to_apply=%region_13.0 | all-reduce | flops 2048 | bytes 16384 | tf_op jit(solution)/shard_map/psum | solution.py:29
  239.6 7.2 %multiply_reduce_fusion = f32[2048]{0:T(1024)S(1)} fusion(f32[2048]{0:T(1024)S(1)} %broadcast_divide_fusion, f32[2048]{0:T(1024)S(1)} %psum.53, f32[2048,2048]{0,1:T(8,128)} %get-tuple-element.6, f32[2048]{0:T(1024)S(1)} %broadcast_divide_fusion.1), kind=kLoop, calls=%fused_computation.2 | loop fusion | flops 16775168 | bytes 16809984 | tf_op jit(solution)/shard_map/reduce_sum | solution.py:32
  246.8 5.0 %psum.55 = f32[2048]{0:T(1024)S(1)} all-reduce(f32[2048]{0:T(1024)S(1)} %multiply_reduce_fusion), channel_id=1, replica_groups=mesh['rows'=16,'cent'=2] {'cent'}, use_global_device_ids=true, to_apply=%region_15.0 | all-reduce | flops 2048 | bytes 16384 | tf_op jit(solution)/shard_map/psum | solution.py:32
  251.8 15.7 %fusion.3 = f32[1024,2048]{0,1:T(8,128)} fusion(bf16[2048,1024]{1,0:T(8,128)(2,1)} %param.2, f32[2048]{0:T(1024)S(1)} %psum.55, f32[2048]{0:T(1024)S(1)} %broadcast_divide_fusion, f32[2048,2048]{0,1:T(8,128)} %get-tuple-element.6, f32[2048]{0:T(1024)S(1)} %psum.53, f32[2048]{0:T(1024)S(1)} %broadcast_divide_fusion.1), kind=kOutput, calls=%fused_computation.11 | convolution fusion | flops 8610906112 | bytes 29392896 | tf_op jit(solution)/shard_map/dot_general | solution.py:38
  267.5 9.1 %copy.6 = f32[1024,2048]{1,0:T(8,128)} copy(f32[1024,2048]{0,1:T(8,128)} %fusion.3) | data formatting | bytes 16777216
  276.6 0.0 reduce-scatter.4.cloned.1.call-update
  276.6 100.9 %reduce-scatter.4.cloned.1.call-done = f32[64,2048]{1,0:T(8,128)} async-done(((f32[1024,2048]{1,0:T(8,128)}), f32[64,2048]{1,0:T(8,128)}) %reduce-scatter.4.cloned.1.call-update) | async-done | bytes 524304 | tf_op jit(solution)/shard_map/reduce_scatter | solution.py:37
  377.5 1.9 broadcast_multiply_fusion
  (3 shorter events, 0.0 us)
Async XLA Ops:
  6.5 56.1 %all-gather.2.cloned.1.call-start = ((), (), s32[]{:S(2)}) async-start(), calls=%async_computation.1 | async-start | bytes 4456448 | tf_op jit(solution)/shard_map/all_gather | solution.py:18
  7.3 370.3 %reduce-scatter.4.cloned.1.call-start = ((), (), s32[]{:S(2)}) async-start(), calls=%async_computation.2 | async-start | bytes 8912896 | tf_op jit(solution)/shard_map/reduce_scatter | solution.py:37
Sparse Core Ops, SparseCore 0:
  9.5 53.0 all-gather.1
  276.7 100.7 reduce-scatter.3
where the time goes:
time: 387 us; the launch traced here: 386 us
  waiting for transfers between devices  157 us (41%)
  blocking collectives  115 us (30%)
  other arithmetic  60.6 us (16%)
  matrix products  30.9 us (8%)
  between operations  13.5 us (3%)
  local copies, waits for them, and re-layouts  9.11 us (2%)
    reduce_scatter x1, waiting for transfers between devices, on_device(): lax.psum_scatter(lax.dot_general(window, weights, (((0,), (0,)), ((), ())...  101 us
    psum x3, blocking collectives, on_device(): column_mass = lax.psum(column_sum, 'rows')  90.2 us
    all_gather x1, waiting for transfers between devices, on_device(): lax.all_gather(centroids, 'rows', axis=0, tiled=True)  55.3 us
    reduce_sum x3, other arithmetic, on_device(): column_sum = jnp.sum(balanced, axis=0)  27.9 us
    reduce_sum x3, other arithmetic, on_device(): row_mass = lax.psum(jnp.sum(balanced, axis=1), 'cent')  22.3 us
    dot_general x1, matrix products, on_device(): lax.dot_general(window, weights, (((0,), (0,)), ((), ())), preferred_elem...  15.7 us
    dot_general x1, matrix products, on_device(): jnp.dot(window, lax.all_gather(centroids, 'rows', axis=0, tiled=True), pr...  15.2 us
    psum x3, blocking collectives, on_device(): row_mass = lax.psum(jnp.sum(balanced, axis=1), 'cent')  15 us
  transfers between devices with their start and end apart: 2, of which 2 were waited for; matrix products, arithmetic and copies ran while one was open for 0% of the time, Pallas kernels for 0%

commit v1 on v0

--- a/solution.py
+++ b/solution.py
@@ -7,6 +7,14 @@
 K = 4096
 ITERS = 3
 sharpness = 3.0
+
+
+def added_up(value, mesh_axis):
+    size, total = (lax.axis_size(mesh_axis), value)
+    for reach in [1 << k for k in range(size.bit_length() - 1)]:
+        swap = [(i, i ^ reach) for i in range(size)]
+        total = total + lax.ppermute(total, mesh_axis, swap)
+    return total
 
 
 def on_device(vectors, centroids):
@@ -26,7 +34,7 @@
     target = row_count * lax.axis_size("rows") / K
     for iteration in range(ITERS):
         column_sum = jnp.sum(balanced, axis=0)
-        column_mass = lax.psum(column_sum, "rows")
+        column_mass = added_up(column_sum, "rows")
         column_scale = target / column_mass
         balanced = balanced * column_scale[None, :]
         row_mass = lax.psum(jnp.sum(balanced, axis=1), "cent")

time: 387 us -> 337 us (0.87)
  blocking collectives: 115 us -> 25 us
  waiting for transfers between devices: 157 us -> 186 us
  starting transfers between devices: 0.04 us -> 11.9 us
    psum x3 -> x0, blocking collectives: 90.2 us -> none  [on_device(): column_mass = lax.psum(column_sum, 'rows')]
    ppermute x0 -> x12, waiting for transfers between devices: none -> 27.3 us  [added_up(): total = total + lax.ppermute(total, mesh_axis, swap)]
    ppermute x0 -> x12, starting transfers between devices: none -> 11.9 us  [added_up(): total = total + lax.ppermute(total, mesh_axis, swap)]
  transfers between devices with their start and end apart: 2 -> 14, of which waited for: 2 -> 14; matrix products, arithmetic and copies ran while one was open for 0% -> 0% of each run, Pallas kernels for 0% -> 0%
where the time goes in v1:
time: 337 us
  waiting for transfers between devices  186 us (55%)
  other arithmetic  60.6 us (18%)
  matrix products  30.9 us (9%)
  blocking collectives  25 us (7%)
  between operations  13.5 us (4%)
  starting transfers between devices  11.9 us (4%)
  local copies, waits for them, and re-layouts  9.11 us (3%)
    reduce_scatter x1, waiting for transfers between devices, on_device(): lax.psum_scatter(lax.dot_general(window, weights, (((0,), (0,)), ((), ())...  102 us
    all_gather x1, waiting for transfers between devices, on_device(): lax.all_gather(centroids, 'rows', axis=0, tiled=True)  55.3 us
    reduce_sum x3, other arithmetic, on_device(): column_sum = jnp.sum(balanced, axis=0)  27.9 us
    ppermute x12, waiting for transfers between devices, added_up(): total = total + lax.ppermute(total, mesh_axis, swap)  27.3 us
    reduce_sum x3, other arithmetic, on_device(): row_mass = lax.psum(jnp.sum(balanced, axis=1), 'cent')  22.3 us
    dot_general x1, matrix products, on_device(): lax.dot_general(window, weights, (((0,), (0,)), ((), ())), preferred_elem...  15.7 us
    dot_general x1, matrix products, on_device(): jnp.dot(window, lax.all_gather(centroids, 'rows', axis=0, tiled=True), pr...  15.2 us
    psum x3, blocking collectives, on_device(): row_mass = lax.psum(jnp.sum(balanced, axis=1), 'cent')  15 us
  transfers between devices with their start and end apart: 14, of which 14 were waited for; matrix products, arithmetic and copies ran while one was open for 0% of the time, Pallas kernels for 0%

profile of v1, /device:TPU:0, one launch (start us, length us, event | category | flops | bytes accessed | tf_op | source)
XLA Modules:
  0.0 336.5 jit_solution(1858010201267054964)
XLA Ops:
  6.5 0.0 all-gather.2.cloned.1.call-start
  6.5 0.7 all-gather.2.cloned.1.call-update
  7.3 0.0 reduce-scatter.4.cloned.1.call-start
  7.3 55.3 %all-gather.2.cloned.1.call-done = bf16[1024,2048]{1,0:T(8,128)(2,1)} async-done(((bf16[64,2048]{1,0:T(8,128)(2,1)}), bf16[1024,2048]{1,0:T(8,128)(2,1)}) %all-gather.2.cloned.1.call-update) | async-done | bytes 4194320 | tf_op jit(solution)/shard_map/all_gather | solution.py:26
  62.6 15.2 %multiply_reduce_fusion.3 = (f32[2048]{0:T(1024)S(1)}, f32[2048,2048]{0,1:T(8,128)}) fusion(bf16[2048,1024]{1,0:T(8,128)(2,1)} %param.2, bf16[1024,2048]{1,0:T(8,128)(2,1)} %all-gather.2.cloned.1.call-done), kind=kOutput, calls=%fused_computation.7 | convolution fusion | flops 8598321152 | bytes 25174016 | tf_op jit(solution)/shard_map/dot_general | solution.py:24
  77.9 5.0 %pmax.7 = f32[2048]{0:T(1024)S(1)} all-reduce(f32[2048]{0:T(1024)S(1)} %get-tuple-element.7), channel_id=1, replica_groups=mesh['rows'=16,'cent'=2] {'cent'}, use_global_device_ids=true, to_apply=%region_1.0 | all-reduce | flops 2048 | bytes 16384 | tf_op jit(solution)/shard_map/pmax | solution.py:30
  82.8 8.5 %fusion.1 = f32[2048]{0:T(1024)S(1)} fusion(f32[2048,2048]{0,1:T(8,128)} %get-tuple-element.8, f32[2048]{0:T(1024)S(1)} %pmax.7), kind=kLoop, calls=%fused_computation.9 | loop fusion | flops 12580864 | bytes 16793600 | tf_op jit(solution)/shard_map/reduce_sum | solution.py:32
  91.4 5.0 %psum.28 = f32[2048]{0:T(1024)S(1)} all-reduce(f32[2048]{0:T(1024)S(1)} %fusion.1), channel_id=1, replica_groups=mesh['rows'=16,'cent'=2] {'cent'}, use_global_device_ids=true, to_apply=%region_3.0 | all-reduce | flops 2048 | bytes 16384 | tf_op jit(solution)/shard_map/psum | solution.py:32
  96.4 7.7 %fusion.4 = f32[2048]{0:T(1024)S(1)} fusion(f32[2048]{0:T(1024)S(1)} %psum.28, f32[2048]{0:T(1024)S(1)} %pmax.7, f32[2048,2048]{0,1:T(8,128)} %get-tuple-element.8), kind=kLoop, calls=%fused_computation.16 | loop fusion | flops 16775168 | bytes 16801792 | tf_op jit(solution)/shard_map/reduce_sum | solution.py:36
  104.1 0.1 collective-permute-start
  104.2 1.2 collective-permute-done
  105.3 0.6 collective-permute-start.1
  105.9 3.1 collective-permute-done.1
  109.0 1.5 collective-permute-start.2
  110.5 2.1 collective-permute-done.2
  112.6 1.8 collective-permute-start.3
  114.5 2.7 collective-permute-done.3
  117.2 8.1 %multiply_reduce_fusion.2 = f32[2048]{0:T(1024)S(1)} fusion(f32[2048]{0:T(1024)S(1)} %add_divide_fusion.2, f32[2048]{0:T(1024)S(1)} %psum.28, f32[2048]{0:T(1024)S(1)} %pmax.7, f32[2048,2048]{0,1:T(8,128)} %get-tuple-element.8), kind=kLoop, calls=%fused_computation.6 | loop fusion | flops 20969472 | bytes 16809984 | tf_op jit(solution)/shard_map/reduce_sum | solution.py:40
  125.3 5.0 %psum.29 = f32[2048]{0:T(1024)S(1)} all-reduce(f32[2048]{0:T(1024)S(1)} %multiply_reduce_fusion.2), channel_id=1, replica_groups=mesh['rows'=16,'cent'=2] {'cent'}, use_global_device_ids=true, to_apply=%region_6.0 | all-reduce | flops 2048 | bytes 16384 | tf_op jit(solution)/shard_map/psum | solution.py:40
  130.3 13.1 %fusion.6 = (f32[2048]{0:T(1024)S(1)}, f32[2048,2048]{0,1:T(8,128)}) fusion(f32[2048]{0:T(1024)S(1)} %psum.29, f32[2048]{0:T(1024)S(1)} %add_divide_fusion.2, f32[2048]{0:T(1024)S(1)} %psum.28, f32[2048]{0:T(1024)S(1)} %pmax.7, f32[2048,2048]{0,1:T(8,128)} %get-tuple-element.8), kind=kLoop, calls=%fused_computation.18 | loop fusion | flops 25163776 | bytes 33595392 | tf_op jit(solution)/shard_map/reduce_sum | solution.py:36
  143.4 0.0 collective-permute-start.4
  143.4 1.2 collective-permute-done.4
  144.6 0.6 collective-permute-start.5
  145.1 3.1 collective-permute-done.5
  148.2 1.5 collective-permute-start.6
  149.8 2.1 collective-permute-done.6
  151.9 1.8 collective-permute-start.7
  153.7 2.7 collective-permute-done.7
  156.5 6.9 %multiply_reduce_fusion.1 = f32[2048]{0:T(1024)S(1)} fusion(f32[2048,2048]{0,1:T(8,128)} %get-tuple-element.6, f32[2048]{0:T(1024)S(1)} %add_divide_fusion.1), kind=kLoop, calls=%fused_computation.4 | loop fusion | flops 8386560 | bytes 16793600 | tf_op jit(solution)/shard_map/reduce_sum | solution.py:40
  163.4 5.0 %psum.30 = f32[2048]{0:T(1024)S(1)} all-reduce(f32[2048]{0:T(1024)S(1)} %multiply_reduce_fusion.1), channel_id=1, replica_groups=mesh['rows'=16,'cent'=2] {'cent'}, use_global_device_ids=true, to_apply=%region_9.0 | all-reduce | flops 2048 | bytes 16384 | tf_op jit(solution)/shard_map/psum | solution.py:40
  168.4 7.1 %fusion.5 = f32[2048]{0:T(1024)S(1)} fusion(f32[2048]{0:T(1024)S(1)} %psum.30, f32[2048,2048]{0,1:T(8,128)} %get-tuple-element.6, f32[2048]{0:T(1024)S(1)} %add_divide_fusion.1), kind=kLoop, calls=%fused_computation.17 | loop fusion | flops 12580864 | bytes 16801792 | tf_op jit(solution)/shard_map/reduce_sum | solution.py:36
  175.5 0.1 collective-permute-start.8
  175.6 1.2 collective-permute-done.8
  176.8 0.6 collective-permute-start.9
  177.3 3.1 collective-permute-done.9
  180.4 1.5 collective-permute-start.10
  182.0 2.1 collective-permute-done.10
  184.1 1.8 collective-permute-start.11
  185.9 2.7 collective-permute-done.11
  188.6 7.2 %multiply_reduce_fusion = f32[2048]{0:T(1024)S(1)} fusion(f32[2048]{0:T(1024)S(1)} %add_divide_fusion, f32[2048]{0:T(1024)S(1)} %psum.30, f32[2048,2048]{0,1:T(8,128)} %get-tuple-element.6, f32[2048]{0:T(1024)S(1)} %add_divide_fusion.1), kind=kLoop, calls=%fused_computation.2 | loop fusion | flops 16775168 | bytes 16809984 | tf_op jit(solution)/shard_map/reduce_sum | solution.py:40
  195.9 5.0 %psum.31 = f32[2048]{0:T(1024)S(1)} all-reduce(f32[2048]{0:T(1024)S(1)} %multiply_reduce_fusion), channel_id=1, replica_groups=mesh['rows'=16,'cent'=2] {'cent'}, use_global_device_ids=true, to_apply=%region_12.0 | all-reduce | flops 2048 | bytes 16384 | tf_op jit(solution)/shard_map/psum | solution.py:40
  200.9 15.7 %fusion.3 = f32[1024,2048]{0,1:T(8,128)} fusion(bf16[2048,1024]{1,0:T(8,128)(2,1)} %param.2, f32[2048]{0:T(1024)S(1)} %psum.31, f32[2048]{0:T(1024)S(1)} %add_divide_fusion, f32[2048,2048]{0,1:T(8,128)} %get-tuple-element.6, f32[2048]{0:T(1024)S(1)} %psum.30, f32[2048]{0:T(1024)S(1)} %add_divide_fusion.1), kind=kOutput, calls=%fused_computation.11 | convolution fusion | flops 8610906112 | bytes 29392896 | tf_op jit(solution)/shard_map/dot_general | solution.py:46
  216.5 9.1 %copy.6 = f32[1024,2048]{1,0:T(8,128)} copy(f32[1024,2048]{0,1:T(8,128)} %fusion.3) | data formatting | bytes 16777216
  225.6 0.0 reduce-scatter.4.cloned.1.call-update
  225.7 102.2 %reduce-scatter.4.cloned.1.call-done = f32[64,2048]{1,0:T(8,128)} async-done(((f32[1024,2048]{1,0:T(8,128)}), f32[64,2048]{1,0:T(8,128)}) %reduce-scatter.4.cloned.1.call-update) | async-done | bytes 524304 | tf_op jit(solution)/shard_map/reduce_scatter | solution.py:45
  327.8 1.9 broadcast_multiply_fusion
  (12 shorter events, 0.0 us)
Async XLA Ops:
  6.5 56.1 %all-gather.2.cloned.1.call-start = ((), (), s32[]{:S(2)}) async-start(), calls=%async_computation.1 | async-start | bytes 4456448 | tf_op jit(solution)/shard_map/all_gather | solution.py:26
  7.3 320.6 %reduce-scatter.4.cloned.1.call-start = ((), (), s32[]{:S(2)}) async-start(), calls=%async_computation.2 | async-start | bytes 8912896 | tf_op jit(solution)/shard_map/reduce_scatter | solution.py:45
  104.1 1.2 collective-permute-start
  105.3 3.7 %collective-permute-start.1 = (f32[2048]{0:T(1024)S(1)}, f32[2048]{0:T(1024)S(1)}, u32[]{:S(2)}, u32[]{:S(2)}) collective-permute-start(f32[2048]{0:T(1024)S(1)} %add.46), channel_id=1, source_target_pairs={{0,4},{2,6},{4,0},{6,2},{8,12},{10,14},{12,8},{14,10},{16,20},{18,... | collective-permute-start | bytes 24584 | tf_op jit(solution)/shard_map/ppermute | solution.py:16
  109.0 3.7 %collective-permute-start.2 = (f32[2048]{0:T(1024)S(1)}, f32[2048]{0:T(1024)S(1)}, u32[]{:S(2)}, u32[]{:S(2)}) collective-permute-start(f32[2048]{0:T(1024)S(1)} %add.47), channel_id=1, source_target_pairs={{0,8},{2,10},{4,12},{6,14},{8,0},{10,2},{12,4},{14,6},{16,24},{18,... | collective-permute-start | bytes 24584 | tf_op jit(solution)/shard_map/ppermute | solution.py:16
  112.6 4.5 %collective-permute-start.3 = (f32[2048]{0:T(1024)S(1)}, f32[2048]{0:T(1024)S(1)}, u32[]{:S(2)}, u32[]{:S(2)}) collective-permute-start(f32[2048]{0:T(1024)S(1)} %add.48), channel_id=1, source_target_pairs={{0,16},{2,18},{4,20},{6,22},{8,24},{10,26},{12,28},{14,30},{16,0},... | collective-permute-start | bytes 24584 | tf_op jit(solution)/shard_map/ppermute | solution.py:16
  143.4 1.2 collective-permute-start.4
  144.6 3.7 %collective-permute-start.5 = (f32[2048]{0:T(1024)S(1)}, f32[2048]{0:T(1024)S(1)}, u32[]{:S(2)}, u32[]{:S(2)}) collective-permute-start(f32[2048]{0:T(1024)S(1)} %add.50), channel_id=1, source_target_pairs={{0,4},{2,6},{4,0},{6,2},{8,12},{10,14},{12,8},{14,10},{16,20},{18,... | collective-permute-start | bytes 24584 | tf_op jit(solution)/shard_map/ppermute | solution.py:16
  148.2 3.7 %collective-permute-start.6 = (f32[2048]{0:T(1024)S(1)}, f32[2048]{0:T(1024)S(1)}, u32[]{:S(2)}, u32[]{:S(2)}) collective-permute-start(f32[2048]{0:T(1024)S(1)} %add.51), channel_id=1, source_target_pairs={{0,8},{2,10},{4,12},{6,14},{8,0},{10,2},{12,4},{14,6},{16,24},{18,... | collective-permute-start | bytes 24584 | tf_op jit(solution)/shard_map/ppermute | solution.py:16
  151.9 4.5 %collective-permute-start.7 = (f32[2048]{0:T(1024)S(1)}, f32[2048]{0:T(1024)S(1)}, u32[]{:S(2)}, u32[]{:S(2)}) collective-permute-start(f32[2048]{0:T(1024)S(1)} %add.52), channel_id=1, source_target_pairs={{0,16},{2,18},{4,20},{6,22},{8,24},{10,26},{12,28},{14,30},{16,0},... | collective-permute-start | bytes 24584 | tf_op jit(solution)/shard_map/ppermute | solution.py:16
  175.5 1.2 collective-permute-start.8
  176.8 3.7 %collective-permute-start.9 = (f32[2048]{0:T(1024)S(1)}, f32[2048]{0:T(1024)S(1)}, u32[]{:S(2)}, u32[]{:S(2)}) collective-permute-start(f32[2048]{0:T(1024)S(1)} %add.54), channel_id=1, source_target_pairs={{0,4},{2,6},{4,0},{6,2},{8,12},{10,14},{12,8},{14,10},{16,20},{18,... | collective-permute-start | bytes 24584 | tf_op jit(solution)/shard_map/ppermute | solution.py:16
  180.4 3.7 %collective-permute-start.10 = (f32[2048]{0:T(1024)S(1)}, f32[2048]{0:T(1024)S(1)}, u32[]{:S(2)}, u32[]{:S(2)}) collective-permute-start(f32[2048]{0:T(1024)S(1)} %add.55), channel_id=1, source_target_pairs={{0,8},{2,10},{4,12},{6,14},{8,0},{10,2},{12,4},{14,6},{16,24},{18,... | collective-permute-start | bytes 24584 | tf_op jit(solution)/shard_map/ppermute | solution.py:16
  184.1 4.5 %collective-permute-start.11 = (f32[2048]{0:T(1024)S(1)}, f32[2048]{0:T(1024)S(1)}, u32[]{:S(2)}, u32[]{:S(2)}) collective-permute-start(f32[2048]{0:T(1024)S(1)} %add.56), channel_id=1, source_target_pairs={{0,16},{2,18},{4,20},{6,22},{8,24},{10,26},{12,28},{14,30},{16,0},... | collective-permute-start | bytes 24584 | tf_op jit(solution)/shard_map/ppermute | solution.py:16
Sparse Core Ops, SparseCore 0:
  9.5 53.0 all-gather.1
  225.8 102.0 reduce-scatter.3
